TPU v7x, 128 devices: a whole 4x4x4 slice. The times are simulated.
128 devices in a mesh: pts: 8 (over x, core), snap: 16 (over z, y).
Axes of the slice: x: 4, y: 4, z: 4, core: 2. Of those that a mesh axis runs over, the one named last changes fastest.
Arguments:
- snapshots: bfloat16 [1024, 3, 65536], P('snap', None, 'pts')
- block_starts: int32 [31], replicated, may hold values from 0 to 960, as said below
- point_slab: int32 [65536], P(('pts', 'snap')), may hold values from 0 to 15
- slab_weight: float32 [16], replicated, may hold values from 1 to 10
Outputs:
- mode_field: bfloat16 [2, 33, 31, 3, 65536], P(None, None, None, None, ('pts', 'snap'))
- r_factor: float32 [2, 33, 31, 31], replicated
Inputs may be any that keep to these rules, and one draw needn't show every extreme that they name: `block_starts`: strictly increasing; the first is 0 and the last is 960; neighbours lie more than 16 apart.
All inputs are finite; a program needn't handle non-finite values.
Results may differ from a plain program's by a relative error of at most 0.0017.
The roundings to bfloat16 on the way count: a program that leaves them out, or rounds other values in their place, can miss the bound.
Values may be sent and summed in bfloat16 or wider, within the bound.
No kernel may reach another device: no remote copies, remote signals or barrier semaphores. Data moves between devices by JAX's collectives and lax.ppermute only.
A program may use at most 128 MiB of HBM per device.

v0:
```python
import math
import jax
import jax.numpy as jnp
from jax import lax
from jax.sharding import PartitionSpec as P

NT = 1024
WIN = 64


def make_tables(length, freq_count):
    steps_time = jnp.arange(length, dtype=jnp.int32)
    freq_index = jnp.arange(freq_count, dtype=jnp.int32)
    phase_index = freq_index[:, None] * steps_time[None, :] % length
    angle_value = 2.0 * math.pi / length * phase_index.astype(jnp.float32)
    window = 0.5 - 0.5 * jnp.cos(2.0 * math.pi / length * steps_time.astype(jnp.float32))
    dft_table = jnp.stack(
        [window[None, :] * jnp.cos(angle_value), -window[None, :] * jnp.sin(angle_value)]
    ).astype(jnp.bfloat16)
    row_sums = jnp.sum(dft_table.astype(jnp.float32), axis=2)
    return (dft_table, row_sums)


def spectra(series, starts, dft_table, row_sums):
    blocks = jax.vmap(lambda offset: lax.dynamic_slice_in_dim(series, offset, WIN, 0))(starts)
    raw_spec = jnp.einsum("kfw,bwcp->kfbcp", dft_table, blocks, preferred_element_type=jnp.float32)
    time_mean = jnp.sum(series.astype(jnp.float32), axis=0) / NT
    return raw_spec - row_sums[:, :, None, None, None] * time_mean[None, None, None]


def gram(amplitude):
    highest = lax.Precision.HIGHEST
    amp_real, amp_imag = (amplitude[0], amplitude[1])
    part_real = jnp.einsum("fbn,fdn->bdf", amp_real, amp_real, precision=highest) + jnp.einsum(
        "fbn,fdn->bdf", amp_imag, amp_imag, precision=highest
    )
    part_imag = jnp.einsum("fbn,fdn->bdf", amp_real, amp_imag, precision=highest) - jnp.einsum(
        "fbn,fdn->bdf", amp_imag, amp_real, precision=highest
    )
    return (part_real, part_imag)


def complex_cholesky(gram_real, gram_imag):
    size_n = gram_real.shape[0]
    positions = jnp.arange(size_n, dtype=jnp.int32)
    rows_real = []
    rows_imag = []
    for column in range(size_n):
        rest_real = gram_real[column]
        rest_imag = gram_imag[column]
        if column > 0:
            done_real = jnp.stack(rows_real)
            done_imag = jnp.stack(rows_imag)
            above_real = done_real[:, column]
            above_imag = done_imag[:, column]
            rest_real = rest_real - jnp.sum(
                above_real[:, None] * done_real + above_imag[:, None] * done_imag, axis=0
            )
            rest_imag = rest_imag - jnp.sum(
                above_real[:, None] * done_imag - above_imag[:, None] * done_real, axis=0
            )
        pivot_value = jnp.sqrt(rest_real[column])
        keep_real = (positions >= column)[:, None]
        keep_imag = (positions > column)[:, None]
        rows_real.append(jnp.where(keep_real, rest_real / pivot_value, jnp.zeros_like(rest_real)))
        rows_imag.append(jnp.where(keep_imag, rest_imag / pivot_value, jnp.zeros_like(rest_imag)))
    return (jnp.stack(rows_real), jnp.stack(rows_imag))


def upper_inverse(upper_real, upper_imag):
    size_n = upper_real.shape[0]
    identity = jnp.eye(size_n, dtype=upper_real.dtype)
    rows_real = []
    rows_imag = []
    for row_index in reversed(range(size_n)):
        rest_real = jnp.broadcast_to(identity[row_index][:, None], upper_real.shape[1:])
        rest_imag = jnp.zeros_like(rest_real)
        if row_index < size_n - 1:
            done_real = jnp.stack(rows_real[::-1])
            done_imag = jnp.stack(rows_imag[::-1])
            coef_real = upper_real[row_index, row_index + 1 :]
            coef_imag = upper_imag[row_index, row_index + 1 :]
            rest_real = rest_real - jnp.sum(
                coef_real[:, None] * done_real - coef_imag[:, None] * done_imag, axis=0
            )
            rest_imag = rest_imag - jnp.sum(
                coef_real[:, None] * done_imag + coef_imag[:, None] * done_real, axis=0
            )
        pivot_value = upper_real[row_index, row_index]
        rows_real.append(rest_real / pivot_value)
        rows_imag.append(rest_imag / pivot_value)
    return (jnp.stack(rows_real[::-1]), jnp.stack(rows_imag[::-1]))


def project(amplitude, inv_real, inv_imag):
    highest = lax.Precision.HIGHEST
    amp_real, amp_imag = (amplitude[0], amplitude[1])
    mode_real = jnp.einsum("fbn,bmf->fmn", amp_real, inv_real, precision=highest) - jnp.einsum(
        "fbn,bmf->fmn", amp_imag, inv_imag, precision=highest
    )
    mode_imag = jnp.einsum("fbn,bmf->fmn", amp_real, inv_imag, precision=highest) + jnp.einsum(
        "fbn,bmf->fmn", amp_imag, inv_real, precision=highest
    )
    return jnp.stack([mode_real, mode_imag])


def on_device(snapshots, block_starts, point_slab, slab_weight):
    dft_table, row_sums = make_tables(WIN, WIN // 2 + 1)
    series = lax.all_to_all(snapshots, "snap", split_axis=2, concat_axis=0, tiled=True)
    spectrum = spectra(series, block_starts, dft_table, row_sums)
    freq_count = spectrum.shape[1]
    block_count = spectrum.shape[2]
    points = spectrum.shape[4]
    all_points = points * lax.axis_size("pts") * lax.axis_size("snap")
    slab_ids = jnp.arange(slab_weight.shape[0], dtype=jnp.int32)
    one_hot = (point_slab[:, None] == slab_ids[None, :]).astype(jnp.float32)
    weights = jnp.dot(one_hot, slab_weight, precision=lax.Precision.HIGHEST)
    root_weight = jnp.sqrt(weights / (0.375 * WIN))
    amplitude = (spectrum * root_weight).reshape(2, freq_count, block_count, 3 * points)
    part_real, part_imag = gram(amplitude)
    norm_scale = 1.0 / (3.0 * all_points)
    sum_real, sum_imag = lax.psum((part_real, part_imag), ("pts", "snap"))
    upper_real, upper_imag = complex_cholesky(sum_real * norm_scale, sum_imag * norm_scale)
    inv_real, inv_imag = upper_inverse(upper_real, upper_imag)
    mode_field = (
        project(amplitude, inv_real, inv_imag)
        .reshape(2, freq_count, block_count, 3, points)
        .astype(jnp.bfloat16)
    )
    r_factor = jnp.transpose(jnp.stack([upper_real, upper_imag]), (0, 3, 1, 2))
    return (mode_field, r_factor)


def solution(mesh):
    in_specs = (P("snap", None, "pts"), P(), P(("pts", "snap")), P())
    out_specs = (P(None, None, None, None, ("pts", "snap")), P())
    return jax.shard_map(
        on_device, mesh=mesh, in_specs=in_specs, out_specs=out_specs, check_vma=False
    )
```

profile of v0, /device:TPU:1, one launch (start us, length us, event | category | flops | bytes accessed | tf_op | source)
XLA Modules:
  0.0 542.6 jit_solution(6044256804985214735)
XLA Ops:
  7.2 11.3 %copy.17234 = bf16[64,3,8192]{0,1,2:T(4,128)(2,1)} copy(bf16[64,3,8192]{2,0,1:T(8,128)(2,1)} %param.4) | data formatting | bytes 6291456 | tf_op args[0]
  18.4 13.4 %reshape.4626 = bf16[16,2,49152]{2,1,0:T(2,128)(2,1)} reshape(bf16[8192,3,64]{2,1,0:T(4,128)(2,1)} %bitcast.635) | data formatting | bytes 6291456
  31.8 8.6 %all-to-all-start = ((bf16[16,2,49152]{2,1,0:T(2,128)(2,1)}), bf16[16,2,49152]{2,1,0:T(2,128)(2,1)S(1)}, u32[]{:S(2)}, u32[]{:S(2)}) async-start(bf16[16,2,49152]{2,1,0:T(2,128)(2,1)} %reshape.4626), calls=%async_computation | async-start | bytes 6291456 | tf_op jit(solution)/shard_map/all_to_all | solution.py:109
  41.5 45.5 %all-to-all-done = bf16[16,2,49152]{2,1,0:T(2,128)(2,1)S(1)} async-done(((bf16[16,2,49152]{2,1,0:T(2,128)(2,1)}), bf16[16,2,49152]{2,1,0:T(2,128)(2,1)S(1)}, u32[]{:S(2)}, u32[]{:S(2)}) %all-to-all-start) | async-done | bytes 3145760 | tf_op jit(solution)/shard_map/all_to_all | solution.py:109
  87.0 9.3 %reshape.4627 = bf16[8192,3,64]{2,1,0:T(4,128)(2,1)} reshape(bf16[16,2,49152]{2,1,0:T(2,128)(2,1)S(1)} %all-to-all-done) | data formatting | bytes 6291456
  96.3 8.3 %copy.17846 = bf16[64,3,16,512]{3,2,0,1:T(8,128)(2,1)S(1)} copy(bf16[64,3,16,512]{0,1,3,2:T(4,128)(2,1)} %bitcast.634) | data formatting | bytes 6291456 | tf_op jit(solution)/shard_map/all_to_all | solution.py:109
  105.4 4.7 copy.17236
  110.2 11.5 %gather_fusion = bf16[31,64,3,512]{3,2,1,0:T(4,128)(2,1)} fusion(bf16[1024,3,512]{2,1,0:T(4,128)(2,1)} %bitcast.633, s32[31]{0:T(128)S(1)} %fusion.108), kind=kCustom, calls=%fused_computation | custom fusion | bytes 12190068 | tf_op jit(solution)/shard_map/vmap()/gather | solution.py:25
  121.7 11.4 %subtract_multiply_fusion = f32[2,33,31,3,512]{4,1,3,2,0:T(8,128)} fusion(f32[512]{0:T(512)S(1)} %multiply_sqrt_fusion, f32[2,33,3,512]{3,1,2,0:T(8,128)S(1)} %broadcast_multiply_fusion.2, bf16[31,64,3,512]{3,2,1,0:T(4,128)(2,1)} %gather_fusion, bf16[1,33,64]{2,1,0:T(8,128)(2,1)S(1)} %get-tuple-element.379, bf16[1,33,64]{2,1,0:T(8,128)(2,1)S(1)} %get-tuple-element.380), kind=kOutput, calls=%fused_computation.1 | convolution fusion | flops 408562176 | bytes 19081472 | tf_op jit(solution)/shard_map/kfw,bwcp->kfbcp/dot_general | solution.py:26
  133.2 12.5 %fusion.116 = (f32[1,33,31,3,512]{4,1,3,2,0:T(8,128)}, f32[1,33,31,3,512]{4,1,3,2,0:T(8,128)}) fusion(f32[2,33,31,3,512]{4,1,3,2,0:T(8,128)} %subtract_multiply_fusion), kind=kLoop, calls=%fused_computation.928 | loop fusion | bytes 25141248 | tf_op jit(solution)/shard_map/slice | solution.py:33
  145.7 10.7 %copy.17238 = f32[1,33,31,3,512]{4,3,2,1,0:T(4,128)} copy(f32[1,33,31,3,512]{4,1,3,2,0:T(8,128)} %get-tuple-element.190) | data formatting | bytes 12570624 | tf_op jit(solution)/shard_map/slice | solution.py:33
  156.4 11.6 %squeeze.62 = f32[33,31,1536]{2,1,0:T(8,128)} reshape(f32[1,33,31,3,512]{4,3,2,1,0:T(4,128)} %copy.17238) | data formatting | bytes 12570624 | tf_op jit(solution)/shard_map/squeeze | solution.py:33
  168.0 10.7 %copy.17239 = f32[1,33,31,3,512]{4,3,2,1,0:T(4,128)} copy(f32[1,33,31,3,512]{4,1,3,2,0:T(8,128)} %get-tuple-element.191) | data formatting | bytes 12570624 | tf_op jit(solution)/shard_map/slice | solution.py:33
  178.7 11.4 %squeeze.63 = f32[33,31,1536]{2,1,0:T(8,128)} reshape(f32[1,33,31,3,512]{4,3,2,1,0:T(4,128)} %copy.17239) | data formatting | bytes 12570624 | tf_op jit(solution)/shard_map/squeeze | solution.py:33
  190.1 9.6 %fusion.123 = f32[33,31,31]{2,1,0:T(8,128)S(1)} fusion(f32[33,31,1536]{2,1,0:T(8,128)} %squeeze.62, f32[33,31,1536]{2,1,0:T(8,128)} %squeeze.63), kind=kOutput, calls=%fused_computation.935 | convolution fusion | flops 584534016 | bytes 12697476 | tf_op jit(solution)/shard_map/fbn,fdn->bdf/dot_general | solution.py:37
  199.8 6.0 %fusion.122 = f32[33,31,31]{2,1,0:T(8,128)S(1)} fusion(f32[33,31,1536]{2,1,0:T(8,128)S(1)} %copy-done.3, f32[33,31,1536]{2,1,0:T(8,128)S(1)} %copy-done.2), kind=kOutput, calls=%fused_computation.934 | convolution fusion | flops 584534016 | bytes 12697476 | tf_op jit(solution)/shard_map/fbn,fdn->bdf/dot_general | solution.py:37
  205.7 6.3 %fusion.120 = f32[33,31,31]{2,1,0:T(8,128)S(1)} fusion(f32[33,31,1536]{2,1,0:T(8,128)S(1)} %copy-done.2), kind=kOutput, calls=%fused_computation.932 | convolution fusion | flops 584534016 | bytes 6412164 | tf_op jit(solution)/shard_map/fbn,fdn->bdf/dot_general | solution.py:34
  212.1 6.1 %fusion.121 = f32[33,31,31]{2,1,0:T(8,128)S(1)} fusion(f32[33,31,1536]{2,1,0:T(8,128)S(1)} %copy-done.3), kind=kOutput, calls=%fused_computation.933 | convolution fusion | flops 584534016 | bytes 6412164 | tf_op jit(solution)/shard_map/fbn,fdn->bdf/dot_general | solution.py:34
  221.9 147.2 %all-reduce.4.cloned.1.call-done = (f32[31,31,33]{2,0,1:T(8,128)}, f32[31,31,33]{2,0,1:T(8,128)}) async-done(((f32[31,31,33]{2,0,1:T(8,128)}, f32[31,31,33]{2,0,1:T(8,128)}), (f32[31,31,33]{2,0,1:T(8,128)}, f32[31,31,33]{2,0,1:T(8,128)})) %all-reduce.4.cloned.1.call-update) | async-done | bytes 253720 | tf_op jit(solution)/shard_map/psum | solution.py:122
  369.1 1.1 broadcast_multiply_fusion.1
  370.2 1.1 broadcast_multiply_fusion
  427.9 1.0 copy.17842
  429.0 2.0 copy.17844
  460.8 0.9 stack.375
  466.4 9.6 %fusion.124 = f32[33,31,1536]{2,1,0:T(8,128)} fusion(f32[31,31,33]{0,1,2:T(8,128)S(1)} %copy.17831, f32[33,31,1536]{2,1,0:T(8,128)} %squeeze.62), kind=kOutput, calls=%fused_computation.936 | convolution fusion | flops 584534016 | bytes 12697476 | tf_op jit(solution)/shard_map/fbn,bmf->fmn/dot_general | solution.py:98
  477.5 9.6 %fusion.125 = f32[33,31,1536]{2,1,0:T(8,128)} fusion(f32[31,31,33]{0,1,2:T(8,128)S(1)} %copy.17835, f32[33,31,1536]{2,1,0:T(8,128)} %squeeze.62), kind=kOutput, calls=%fused_computation.937 | convolution fusion | flops 584534016 | bytes 12697476 | tf_op jit(solution)/shard_map/fbn,bmf->fmn/dot_general | solution.py:101
  487.0 9.6 %subtract_convert_fusion = bf16[33,31,1536]{2,1,0:T(8,128)(2,1)} fusion(f32[33,31,1536]{2,1,0:T(8,128)S(1)} %bitcast.638, f32[31,31,33]{0,1,2:T(8,128)S(1)} %copy.17835, f32[33,31,1536]{2,1,0:T(8,128)} %squeeze.63), kind=kOutput, calls=%fused_computation.4 | convolution fusion | flops 587676672 | bytes 15840132 | tf_op jit(solution)/shard_map/fbn,bmf->fmn/dot_general | solution.py:98
  496.6 8.7 %stack.380 = bf16[1,33,31,3,512]{4,3,2,1,0:T(4,128)(2,1)} reshape(bf16[33,31,1536]{2,1,0:T(8,128)(2,1)} %subtract_convert_fusion) | data formatting | bytes 6285312 | tf_op jit(solution)/shard_map/stack | solution.py:104
  505.3 8.9 %add_convert_fusion = bf16[33,31,1536]{2,1,0:T(8,128)(2,1)S(1)} fusion(f32[33,31,1536]{2,1,0:T(8,128)} %fusion.125, f32[31,31,33]{0,1,2:T(8,128)} %copy-done.5, f32[33,31,1536]{2,1,0:T(8,128)} %squeeze.63), kind=kOutput, calls=%fused_computation.3 | convolution fusion | flops 587676672 | bytes 15840132 | tf_op jit(solution)/shard_map/fbn,bmf->fmn/dot_general | solution.py:101
  514.2 5.8 %stack.381 = bf16[1,33,31,3,512]{4,3,2,1,0:T(4,128)(2,1)} reshape(bf16[33,31,1536]{2,1,0:T(8,128)(2,1)S(1)} %add_convert_fusion) | data formatting | bytes 6285312 | tf_op jit(solution)/shard_map/stack | solution.py:104
  520.0 7.6 %pad_maximum_fusion = bf16[2,33,31,3,512]{4,3,2,1,0:T(4,128)(2,1)S(1)} fusion(bf16[1,33,31,3,512]{4,3,2,1,0:T(4,128)(2,1)} %stack.381, bf16[1,33,31,3,512]{4,3,2,1,0:T(4,128)(2,1)} %stack.380), kind=kLoop, calls=%fused_computation.2 | loop fusion | flops 3142656 | bytes 12570624 | tf_op jit(solution)/shard_map/stack | solution.py:104
  527.7 7.6 %copy.17843 = bf16[2,33,31,3,512]{4,0,3,2,1:T(2,128)(2,1)} copy(bf16[2,33,31,3,512]{4,3,2,1,0:T(4,128)(2,1)S(1)} %pad_maximum_fusion) | data formatting | bytes 12570624
  (970 shorter events, 93.5 us)
Async XLA Ops:
  7.2 34.0 %copy-start = (f32[16]{0:T(128)S(1)}, f32[16]{0:T(128)}, u32[]{:S(2)}) copy-start(f32[16]{0:T(128)} %param.7) | copy-start | bytes 196
  18.4 22.7 %copy-start.7 = (s32[31]{0:T(128)S(1)}, s32[31]{0:T(128)}, u32[]{:S(2)}) copy-start(s32[31]{0:T(128)} %param.5) | copy-start | bytes 376
  18.4 22.7 %copy-start.6 = (s32[512]{0:T(512)S(1)}, s32[512]{0:T(512)}, u32[]{:S(2)}) copy-start(s32[512]{0:T(512)} %param.6) | copy-start | bytes 6148
  31.8 55.2 %all-to-all-start = ((bf16[16,2,49152]{2,1,0:T(2,128)(2,1)}), bf16[16,2,49152]{2,1,0:T(2,128)(2,1)S(1)}, u32[]{:S(2)}, u32[]{:S(2)}) async-start(bf16[16,2,49152]{2,1,0:T(2,128)(2,1)} %reshape.4626), calls=%async_computation | async-start | bytes 6291456 | tf_op jit(solution)/shard_map/all_to_all | solution.py:109
  40.4 328.7 %all-reduce.4.cloned.1.call-start = ((), (), s32[]{:S(2)}) async-start(), calls=%async_computation.1 | async-start | bytes 2031616 | tf_op jit(solution)/shard_map/psum | solution.py:122
  190.1 9.6 %copy-start.2 = (f32[33,31,1536]{2,1,0:T(8,128)S(1)}, f32[33,31,1536]{2,1,0:T(8,128)}, u32[]{:S(2)}) copy-start(f32[33,31,1536]{2,1,0:T(8,128)} %squeeze.62) | copy-start | bytes 18855940
  190.1 9.6 %copy-start.3 = (f32[33,31,1536]{2,1,0:T(8,128)S(1)}, f32[33,31,1536]{2,1,0:T(8,128)}, u32[]{:S(2)}) copy-start(f32[33,31,1536]{2,1,0:T(8,128)} %squeeze.63) | copy-start | bytes 18855940
  372.6 54.5 %copy-start.4 = (f32[1,31,33]{2,0,1:T(1,128)}, f32[1,31,33]{2,0,1:T(1,128)S(1)}, u32[]{:S(2)}) copy-start(f32[1,31,33]{2,0,1:T(1,128)S(1)} %broadcast_select_fusion.55) | copy-start | bytes 12280
  452.1 8.1 %slice-start.2 = ((f32[1,31,33]{2,0,1:T(1,128)}), f32[1,28,33]{2,0,1:T(1,128)S(1)}, s32[]{:S(2)}) async-start(f32[1,31,33]{2,0,1:T(1,128)} %copy-done.4), calls=%async_computation.4 | async-start | bytes 28672 | tf_op jit(solution)/shard_map/slice | solution.py:82
  466.4 9.6 %copy-start.5 = (f32[31,31,33]{0,1,2:T(8,128)}, f32[31,31,33]{0,1,2:T(8,128)S(1)}, u32[]{:S(2)}) copy-start(f32[31,31,33]{0,1,2:T(8,128)S(1)} %copy.17831) | copy-start | bytes 380560
  476.8 10.2 %slice-start = ((s8[6488064]{0:T(1024)(128)(4,1)}), s8[2293760]{0:T(1024)(128)(4,1)S(1)}, s32[]{:S(2)}) async-start(s8[6488064]{0:T(1024)(128)(4,1)} %bitcast.637), calls=%async_computation.2 | async-start | bytes 4587520
  477.4 9.6 %slice-start.1 = ((s8[6488064]{0:T(1024)(128)(4,1)}), s8[4194304]{0:T(1024)(128)(4,1)S(1)}, s32[]{:S(2)}) async-start(s8[6488064]{0:T(1024)(128)(4,1)} %bitcast.637), calls=%async_computation.3 | async-start | bytes 8388608
  520.0 15.3 %copy-start.1 = (f32[16]{0:T(128)S(1)}, f32[16]{0:T(128)}, u32[]{:S(2)}) copy-start(f32[16]{0:T(128)} %param.7) | copy-start | bytes 196
Sparse Core Ops, SparseCore 0:
  222.0 147.0 all-reduce.3
where the time goes:
time: 550 us; the launch traced here: 543 us
  local copies, waits for them, and re-layouts  208 us (38%)
  waiting for transfers between devices  193 us (35%)
  matrix products  77.5 us (14%)
  other arithmetic  36.1 us (7%)
  between operations  19.5 us (4%)
  starting transfers between devices  8.64 us (2%)
    psum x1, waiting for transfers between devices, on_device(): sum_real, sum_imag = lax.psum((part_real, part_imag), ('pts', 'snap'))  147 us
    unnamed x352, local copies, waits for them, and re-layouts  52.7 us
    all_to_all x1, waiting for transfers between devices, on_device(): lax.all_to_all(snapshots, 'snap', split_axis=2, concat_axis=0, tiled=True)  45.5 us
    slice x3, local copies, waits for them, and re-layouts, gram(): amp_real, amp_imag = (amplitude[0], amplitude[1])  33.9 us
    squeeze x2, local copies, waits for them, and re-layouts, gram(): amp_real, amp_imag = (amplitude[0], amplitude[1])  23 us
    another operation x2, local copies, waits for them, and re-layouts, project(): return jnp.stack([mode_real, mode_imag])  14.5 us
    all_to_all x2, local copies, waits for them, and re-layouts, on_device(): lax.all_to_all(snapshots, 'snap', split_axis=2, concat_axis=0, tiled=True)  13 us
    another operation x27, local copies, waits for them, and re-layouts, complex_cholesky(): done_real = jnp.stack(rows_real)  11.6 us
  transfers between devices with their start and end apart: 2, of which 2 were waited for; matrix products, arithmetic and copies ran while one was open for 0% of the time, Pallas kernels for 0%

commit v1 on v0

--- a/solution.py
+++ b/solution.py
@@ -106,7 +106,14 @@
 
 def on_device(snapshots, block_starts, point_slab, slab_weight):
     dft_table, row_sums = make_tables(WIN, WIN // 2 + 1)
-    series = lax.all_to_all(snapshots, "snap", split_axis=2, concat_axis=0, tiled=True)
+
+    def lead_strings(q_in, k_dim, dim_k):
+        found_now = lax.psum(1, "snap")
+        a_now = jnp.split(q_in, found_now, k_dim)
+        carry_out = lax.all_to_all(jnp.stack(a_now), "snap", 0, 0)
+        return jnp.concatenate(carry_out, axis=dim_k)
+
+    series = lead_strings(snapshots, 2, 0)
     spectrum = spectra(series, block_starts, dft_table, row_sums)
     freq_count = spectrum.shape[1]
     block_count = spectrum.shape[2]

time: 550 us -> 530 us (0.964)
  local copies, waits for them, and re-layouts: 208 us -> 192 us
    unnamed x352 -> x368, local copies, waits for them, and re-layouts: 52.7 us -> 43.1 us
    all_to_all x2 -> x1, local copies, waits for them, and re-layouts: 13 us -> 4.73 us  [lead_strings(): carry_out = lax.all_to_all(jnp.stack(a_now), 'snap', 0, 0)]
where the time goes in v1:
time: 530 us; the launch traced here: 525 us
  waiting for transfers between devices  193 us (36%)
  local copies, waits for them, and re-layouts  192 us (36%)
  matrix products  75.5 us (14%)
  other arithmetic  36.6 us (7%)
  between operations  19.5 us (4%)
  starting transfers between devices  8.64 us (2%)
    psum x1, waiting for transfers between devices, on_device(): sum_real, sum_imag = lax.psum((part_real, part_imag), ('pts', 'snap'))  147 us
    all_to_all x1, waiting for transfers between devices, lead_strings(): carry_out = lax.all_to_all(jnp.stack(a_now), 'snap', 0, 0)  45.5 us
    unnamed x368, local copies, waits for them, and re-layouts  43.1 us
    slice x3, local copies, waits for them, and re-layouts, gram(): amp_real, amp_imag = (amplitude[0], amplitude[1])  33.9 us
    squeeze x2, local copies, waits for them, and re-layouts, gram(): amp_real, amp_imag = (amplitude[0], amplitude[1])  23 us
    another operation x2, local copies, waits for them, and re-layouts, project(): return jnp.stack([mode_real, mode_imag])  14.5 us
    another operation x27, local copies, waits for them, and re-layouts, complex_cholesky(): done_real = jnp.stack(rows_real)  11.6 us
    gather x1, local copies, waits for them, and re-layouts, spectra(): lax.dynamic_slice_in_dim(series, offset, WIN, 0)  11.6 us
  transfers between devices with their start and end apart: 2, of which 2 were waited for; matrix products, arithmetic and copies ran while one was open for 0% of the time, Pallas kernels for 0%

profile of v1, /device:TPU:1, one launch (start us, length us, event | category | flops | bytes accessed | tf_op | source)
XLA Modules:
  0.0 524.9 jit_solution(7392210767307836956)
XLA Ops:
  7.2 1.6 constant_dynamic-update-slice_fusion.15
  8.8 1.6 constant_dynamic-update-slice_fusion.14
  13.7 1.6 constant_dynamic-update-slice_fusion.11
  16.9 1.6 constant_dynamic-update-slice_fusion.9
  20.1 1.6 constant_dynamic-update-slice_fusion.7
  25.0 1.6 constant_dynamic-update-slice_fusion.4
  26.6 1.6 constant_dynamic-update-slice_fusion.3
  29.8 1.6 constant_dynamic-update-slice_fusion.1
  33.1 8.6 %all-to-all-start = ((bf16[16,64,3,512]{3,1,2,0:T(8,128)(2,1)}), bf16[16,64,3,512]{3,1,2,0:T(8,128)(2,1)S(1)}, u32[]{:S(2)}, u32[]{:S(2)}) async-start(bf16[16,64,3,512]{3,1,2,0:T(8,128)(2,1)} %constant_dynamic-update-slice_fusion), calls=%async_computation | async-start | bytes 6291456 | tf_op jit(solution)/shard_map/all_to_all | solution.py:113
  42.8 45.5 %all-to-all-done = bf16[16,64,3,512]{3,1,2,0:T(8,128)(2,1)S(1)} async-done(((bf16[16,64,3,512]{3,1,2,0:T(8,128)(2,1)}), bf16[16,64,3,512]{3,1,2,0:T(8,128)(2,1)S(1)}, u32[]{:S(2)}, u32[]{:S(2)}) %all-to-all-start) | async-done | bytes 3145760 | tf_op jit(solution)/shard_map/all_to_all | solution.py:113
  89.7 4.7 copy.17230
  94.4 11.6 %gather_fusion = bf16[31,64,3,512]{3,2,1,0:T(4,128)(2,1)} fusion(bf16[1024,3,512]{2,1,0:T(4,128)(2,1)} %bitcast.662, s32[31]{0:T(128)S(1)} %fusion.108), kind=kCustom, calls=%fused_computation | custom fusion | bytes 12190068 | tf_op jit(solution)/shard_map/vmap()/gather | solution.py:25
  106.0 11.4 %subtract_multiply_fusion = f32[2,33,31,3,512]{4,1,3,2,0:T(8,128)} fusion(f32[512]{0:T(512)S(1)} %multiply_sqrt_fusion, f32[2,33,3,512]{3,1,2,0:T(8,128)S(1)} %copy-done.7, bf16[31,64,3,512]{3,2,1,0:T(4,128)(2,1)} %gather_fusion, bf16[1,33,64]{2,1,0:T(8,128)(2,1)S(1)} %get-tuple-element.379, bf16[1,33,64]{2,1,0:T(8,128)(2,1)S(1)} %get-tuple-element.380), kind=kOutput, calls=%fused_computation.1 | convolution fusion | flops 408562176 | bytes 19081472 | tf_op jit(solution)/shard_map/kfw,bwcp->kfbcp/dot_general | solution.py:26
  117.5 12.5 %fusion.116 = (f32[1,33,31,3,512]{4,1,3,2,0:T(8,128)}, f32[1,33,31,3,512]{4,1,3,2,0:T(8,128)}) fusion(f32[2,33,31,3,512]{4,1,3,2,0:T(8,128)} %subtract_multiply_fusion), kind=kLoop, calls=%fused_computation.944 | loop fusion | bytes 25141248 | tf_op jit(solution)/shard_map/slice | solution.py:33
  130.0 10.7 %copy.17232 = f32[1,33,31,3,512]{4,3,2,1,0:T(4,128)} copy(f32[1,33,31,3,512]{4,1,3,2,0:T(8,128)} %get-tuple-element.190) | data formatting | bytes 12570624 | tf_op jit(solution)/shard_map/slice | solution.py:33
  140.7 11.6 %squeeze.62 = f32[33,31,1536]{2,1,0:T(8,128)} reshape(f32[1,33,31,3,512]{4,3,2,1,0:T(4,128)} %copy.17232) | data formatting | bytes 12570624 | tf_op jit(solution)/shard_map/squeeze | solution.py:33
  152.3 10.7 %copy.17233 = f32[1,33,31,3,512]{4,3,2,1,0:T(4,128)} copy(f32[1,33,31,3,512]{4,1,3,2,0:T(8,128)} %get-tuple-element.191) | data formatting | bytes 12570624 | tf_op jit(solution)/shard_map/slice | solution.py:33
  163.0 11.4 %squeeze.63 = f32[33,31,1536]{2,1,0:T(8,128)} reshape(f32[1,33,31,3,512]{4,3,2,1,0:T(4,128)} %copy.17233) | data formatting | bytes 12570624 | tf_op jit(solution)/shard_map/squeeze | solution.py:33
  174.4 9.6 %fusion.123 = f32[33,31,31]{2,1,0:T(8,128)S(1)} fusion(f32[33,31,1536]{2,1,0:T(8,128)} %squeeze.62, f32[33,31,1536]{2,1,0:T(8,128)} %squeeze.63), kind=kOutput, calls=%fused_computation.951 | convolution fusion | flops 584534016 | bytes 12697476 | tf_op jit(solution)/shard_map/fbn,fdn->bdf/dot_general | solution.py:37
  184.0 6.0 %fusion.122 = f32[33,31,31]{2,1,0:T(8,128)S(1)} fusion(f32[33,31,1536]{2,1,0:T(8,128)S(1)} %copy-done.3, f32[33,31,1536]{2,1,0:T(8,128)S(1)} %copy-done.2), kind=kOutput, calls=%fused_computation.950 | convolution fusion | flops 584534016 | bytes 12697476 | tf_op jit(solution)/shard_map/fbn,fdn->bdf/dot_general | solution.py:37
  190.0 6.3 %fusion.120 = f32[33,31,31]{2,1,0:T(8,128)S(1)} fusion(f32[33,31,1536]{2,1,0:T(8,128)S(1)} %copy-done.2), kind=kOutput, calls=%fused_computation.948 | convolution fusion | flops 584534016 | bytes 6412164 | tf_op jit(solution)/shard_map/fbn,fdn->bdf/dot_general | solution.py:34
  196.4 6.1 %fusion.121 = f32[33,31,31]{2,1,0:T(8,128)S(1)} fusion(f32[33,31,1536]{2,1,0:T(8,128)S(1)} %copy-done.3), kind=kOutput, calls=%fused_computation.949 | convolution fusion | flops 584534016 | bytes 6412164 | tf_op jit(solution)/shard_map/fbn,fdn->bdf/dot_general | solution.py:34
  206.2 147.2 %all-reduce.4.cloned.1.call-done = (f32[31,31,33]{2,0,1:T(8,128)}, f32[31,31,33]{2,0,1:T(8,128)}) async-done(((f32[31,31,33]{2,0,1:T(8,128)}, f32[31,31,33]{2,0,1:T(8,128)}), (f32[31,31,33]{2,0,1:T(8,128)}, f32[31,31,33]{2,0,1:T(8,128)})) %all-reduce.4.cloned.1.call-update) | async-done | bytes 253720 | tf_op jit(solution)/shard_map/psum | solution.py:129
  413.3 2.0 copy.17838
  450.7 9.6 %fusion.124 = f32[33,31,1536]{2,1,0:T(8,128)} fusion(f32[31,31,33]{0,1,2:T(8,128)S(1)} %copy.17825, f32[33,31,1536]{2,1,0:T(8,128)} %squeeze.62), kind=kOutput, calls=%fused_computation.952 | convolution fusion | flops 584534016 | bytes 12697476 | tf_op jit(solution)/shard_map/fbn,bmf->fmn/dot_general | solution.py:98
  461.7 9.6 %fusion.125 = f32[33,31,1536]{2,1,0:T(8,128)} fusion(f32[31,31,33]{0,1,2:T(8,128)S(1)} %copy.17829, f32[33,31,1536]{2,1,0:T(8,128)} %squeeze.62), kind=kOutput, calls=%fused_computation.953 | convolution fusion | flops 584534016 | bytes 12697476 | tf_op jit(solution)/shard_map/fbn,bmf->fmn/dot_general | solution.py:101
  471.3 7.6 %subtract_convert_fusion = bf16[33,31,1536]{2,1,0:T(8,128)(2,1)} fusion(f32[33,31,1536]{2,1,0:T(8,128)S(1)} %copy-done.4, f32[31,31,33]{0,1,2:T(8,128)S(1)} %copy.17829, f32[33,31,1536]{2,1,0:T(8,128)S(1)} %bitcast.661), kind=kOutput, calls=%fused_computation.4 | convolution fusion | flops 587676672 | bytes 15840132 | tf_op jit(solution)/shard_map/fbn,bmf->fmn/dot_general | solution.py:98
  478.9 8.7 %stack.431 = bf16[1,33,31,3,512]{4,3,2,1,0:T(4,128)(2,1)} reshape(bf16[33,31,1536]{2,1,0:T(8,128)(2,1)} %subtract_convert_fusion) | data formatting | bytes 6285312 | tf_op jit(solution)/shard_map/stack | solution.py:104
  487.6 8.9 %add_convert_fusion = bf16[33,31,1536]{2,1,0:T(8,128)(2,1)S(1)} fusion(f32[33,31,1536]{2,1,0:T(8,128)} %fusion.125, f32[31,31,33]{0,1,2:T(8,128)} %copy-done.6, f32[33,31,1536]{2,1,0:T(8,128)} %squeeze.63), kind=kOutput, calls=%fused_computation.3 | convolution fusion | flops 587676672 | bytes 15840132 | tf_op jit(solution)/shard_map/fbn,bmf->fmn/dot_general | solution.py:101
  496.6 5.8 %stack.432 = bf16[1,33,31,3,512]{4,3,2,1,0:T(4,128)(2,1)} reshape(bf16[33,31,1536]{2,1,0:T(8,128)(2,1)S(1)} %add_convert_fusion) | data formatting | bytes 6285312 | tf_op jit(solution)/shard_map/stack | solution.py:104
  502.4 7.6 %pad_maximum_fusion = bf16[2,33,31,3,512]{4,3,2,1,0:T(4,128)(2,1)S(1)} fusion(bf16[1,33,31,3,512]{4,3,2,1,0:T(4,128)(2,1)} %stack.432, bf16[1,33,31,3,512]{4,3,2,1,0:T(4,128)(2,1)} %stack.431), kind=kLoop, calls=%fused_computation.2 | loop fusion | flops 3142656 | bytes 12570624 | tf_op jit(solution)/shard_map/stack | solution.py:104
  510.0 7.6 %copy.17837 = bf16[2,33,31,3,512]{4,0,3,2,1:T(2,128)(2,1)} copy(bf16[2,33,31,3,512]{4,3,2,1,0:T(4,128)(2,1)S(1)} %pad_maximum_fusion) | data formatting | bytes 12570624
  (986 shorter events, 111.0 us)
Async XLA Ops:
  7.2 35.2 %copy-start = (f32[16]{0:T(128)S(1)}, f32[16]{0:T(128)}, u32[]{:S(2)}) copy-start(f32[16]{0:T(128)} %param.7) | copy-start | bytes 196
  25.0 17.4 %copy-start.9 = (s32[31]{0:T(128)S(1)}, s32[31]{0:T(128)}, u32[]{:S(2)}) copy-start(s32[31]{0:T(128)} %param.5) | copy-start | bytes 376
  25.0 17.4 %copy-start.8 = (s32[512]{0:T(512)S(1)}, s32[512]{0:T(512)}, u32[]{:S(2)}) copy-start(s32[512]{0:T(512)} %param.6) | copy-start | bytes 6148
  33.1 55.2 %all-to-all-start = ((bf16[16,64,3,512]{3,1,2,0:T(8,128)(2,1)}), bf16[16,64,3,512]{3,1,2,0:T(8,128)(2,1)S(1)}, u32[]{:S(2)}, u32[]{:S(2)}) async-start(bf16[16,64,3,512]{3,1,2,0:T(8,128)(2,1)} %constant_dynamic-update-slice_fusion), calls=%async_computation | async-start | bytes 6291456 | tf_op jit(solution)/shard_map/all_to_all | solution.py:113
  41.7 311.7 %all-reduce.4.cloned.1.call-start = ((), (), s32[]{:S(2)}) async-start(), calls=%async_computation.1 | async-start | bytes 2031616 | tf_op jit(solution)/shard_map/psum | solution.py:129
  94.4 11.6 %copy-start.7 = (f32[2,33,3,512]{3,1,2,0:T(8,128)S(1)}, f32[2,33,3,512]{3,1,2,0:T(8,128)}, u32[]{:S(2)}) copy-start(f32[2,33,3,512]{3,1,2,0:T(8,128)} %broadcast_multiply_fusion.2) | copy-start | bytes 1216516
  174.4 9.6 %copy-start.2 = (f32[33,31,1536]{2,1,0:T(8,128)S(1)}, f32[33,31,1536]{2,1,0:T(8,128)}, u32[]{:S(2)}) copy-start(f32[33,31,1536]{2,1,0:T(8,128)} %squeeze.62) | copy-start | bytes 18855940
  174.4 9.6 %copy-start.3 = (f32[33,31,1536]{2,1,0:T(8,128)S(1)}, f32[33,31,1536]{2,1,0:T(8,128)}, u32[]{:S(2)}) copy-start(f32[33,31,1536]{2,1,0:T(8,128)} %squeeze.63) | copy-start | bytes 18855940
  356.8 54.5 %copy-start.5 = (f32[1,31,33]{2,0,1:T(1,128)}, f32[1,31,33]{2,0,1:T(1,128)S(1)}, u32[]{:S(2)}) copy-start(f32[1,31,33]{2,0,1:T(1,128)S(1)} %broadcast_select_fusion.55) | copy-start | bytes 12280
  439.2 5.3 %slice-start.2 = ((f32[1,31,33]{2,0,1:T(1,128)}), f32[1,28,33]{2,0,1:T(1,128)S(1)}, s32[]{:S(2)}) async-start(f32[1,31,33]{2,0,1:T(1,128)} %copy-done.5), calls=%async_computation.4 | async-start | bytes 28672 | tf_op jit(solution)/shard_map/slice | solution.py:82
  450.7 9.6 %copy-start.6 = (f32[31,31,33]{0,1,2:T(8,128)}, f32[31,31,33]{0,1,2:T(8,128)S(1)}, u32[]{:S(2)}) copy-start(f32[31,31,33]{0,1,2:T(8,128)S(1)} %copy.17825) | copy-start | bytes 380560
  461.1 10.2 %slice-start = ((s8[6488064]{0:T(1024)(128)(4,1)}), s8[2293760]{0:T(1024)(128)(4,1)S(1)}, s32[]{:S(2)}) async-start(s8[6488064]{0:T(1024)(128)(4,1)} %bitcast.660), calls=%async_computation.2 | async-start | bytes 4587520
  461.7 9.6 %slice-start.1 = ((s8[6488064]{0:T(1024)(128)(4,1)}), s8[4194304]{0:T(1024)(128)(4,1)S(1)}, s32[]{:S(2)}) async-start(s8[6488064]{0:T(1024)(128)(4,1)} %bitcast.660), calls=%async_computation.3 | async-start | bytes 8388608
  461.7 9.6 %copy-start.4 = (f32[33,31,1536]{2,1,0:T(8,128)S(1)}, f32[33,31,1536]{2,1,0:T(8,128)}, u32[]{:S(2)}) copy-start(f32[33,31,1536]{2,1,0:T(8,128)} %fusion.124) | copy-start | bytes 18855940
  502.4 15.3 %copy-start.1 = (f32[16]{0:T(128)S(1)}, f32[16]{0:T(128)}, u32[]{:S(2)}) copy-start(f32[16]{0:T(128)} %param.7) | copy-start | bytes 196
Sparse Core Ops, SparseCore 0:
  206.3 147.0 all-reduce.3
